TPU v7x, 128 devices: a whole 4x4x4 slice. The times are simulated.
128 devices in a mesh: energy: 32 (over x, z, core), mom: 4 (over y).
Axes of the slice: x: 4, y: 4, z: 4, core: 2. Of those that a mesh axis runs over, the one named last changes fastest.
Arguments:
- inverse_blocks: bfloat16 [2, 64, 4, 2048, 256], P(None, 'energy', 'mom'), may hold values from -0.25 to 0.25
- coupling_blocks: bfloat16 [2, 4, 2048, 256], P(None, 'mom'), may hold values from -0.10595703 to 0.10595703
- shifts: int32 [4], replicated, may hold values from 0 to 1, as said below
- emission_weight: float32 [4, 4, 4], replicated, may hold values from 0.5 to 4
- absorption_weight: float32 [4, 4, 4], replicated, may hold values from 0.5 to 4
- deform_potential: float32 [2048], replicated, may hold values from 0.5 to 2
- range_rows: int32 [128], replicated, may hold values from 1 to 32, 2048 in all
Outputs:
- sigma: bfloat16 [2, 64, 4, 2048, 256], P(None, 'energy', 'mom')
- charge: float32 [128], P(('energy', 'mom'))
Inputs may be any that keep to these rules, and one draw needn't show every extreme that they name: `shifts`: one mode's shift is exactly 1. `range_rows`: the counts add up to 2048; the largest is exactly 32.
All inputs are finite; a program needn't handle non-finite values.
Results may differ from a plain program's by a relative error of at most 0.015.
Values may be sent and summed in bfloat16 or wider, within the bound.
A program may use at most 192 MiB of HBM per device.

v0:
```python
import jax
import jax.numpy as jnp
from jax import lax
from jax.sharding import PartitionSpec as P

SMAX = 1


HIGH = lax.Precision.HIGHEST


def complex_product(spec, left_re, left_im, right_re, right_im):

    def product(first, second):
        return jnp.einsum(spec, first, second, preferred_element_type=jnp.float32)

    return (
        product(left_re, right_re) - product(left_im, right_im),
        product(left_re, right_im) + product(left_im, right_re),
    )


def solve_chain(inverse_blocks, coupling_blocks):
    energies = inverse_blocks.shape[1]
    width = inverse_blocks.shape[-1]
    nblocks = inverse_blocks.shape[3] // width
    inverse = inverse_blocks[:, :, 0].reshape(2, energies, nblocks, width, width)
    coupled = coupling_blocks[:, 0].reshape(2, nblocks, width, width)
    outputs = []
    green_re = None
    green_im = None
    for block in range(nblocks):
        a_re = inverse[0, :, block]
        a_im = inverse[1, :, block]
        t_re = coupled[0, block]
        t_im = coupled[1, block]
        if block == 0:
            s_re, s_im = complex_product("ij,lj->il", t_re, t_im, t_re, -t_im)
            s_re = jnp.broadcast_to(s_re.astype(jnp.bfloat16)[None], (energies, width, width))
            s_im = jnp.broadcast_to(s_im.astype(jnp.bfloat16)[None], (energies, width, width))
        else:
            p_re, p_im = complex_product("ij,ejk->eik", t_re, t_im, green_re, green_im)
            p_re, p_im = (p_re.astype(jnp.bfloat16), p_im.astype(jnp.bfloat16))
            s_re, s_im = complex_product("eij,lj->eil", p_re, p_im, t_re, -t_im)
            s_re, s_im = (s_re.astype(jnp.bfloat16), s_im.astype(jnp.bfloat16))
        q_re, q_im = complex_product("eij,ejk->eik", a_re, a_im, s_re, s_im)
        q_re, q_im = (q_re.astype(jnp.bfloat16), q_im.astype(jnp.bfloat16))
        h_re, h_im = complex_product("eij,ejk->eik", q_re, q_im, a_re, a_im)
        green_re = (a_re.astype(jnp.float32) + h_re).astype(jnp.bfloat16)
        green_im = (a_im.astype(jnp.float32) + h_im).astype(jnp.bfloat16)
        outputs.append(jnp.stack([green_re, green_im]))
    return jnp.stack(outputs, axis=2).reshape(2, energies, nblocks * width, width)


def fold_weights(shifts, emission, absorption, reach):
    folded = []
    for offset in range(-reach, reach + 1):
        lower_sel = (shifts == -offset).astype(jnp.float32)
        upper_sel = (shifts == offset).astype(jnp.float32)
        weight = jnp.einsum("p,pkq->kq", lower_sel, emission, precision=HIGH)
        weight = weight + jnp.einsum("p,pkq->kq", upper_sel, absorption, precision=HIGH)
        folded.append(weight)
    return jnp.stack(folded)


def shifted_grid(grid, padded, offset):
    e_local = grid.shape[1]
    n_energy = grid.shape[2]
    if offset == 0:
        return grid
    if offset > 0:
        first = padded[:, offset:, 1 : 1 + n_energy]
        second = padded[:, :offset, 2 : 2 + n_energy]
        return jnp.concatenate([first, second], axis=1)
    back_by = -offset
    first = padded[:, e_local - back_by :, 0:n_energy]
    second = padded[:, : e_local - back_by, 1 : 1 + n_energy]
    return jnp.concatenate([first, second], axis=1)


def relayout(slots, forward):
    if forward:
        return lax.all_to_all(slots, ("energy", "mom"), split_axis=2, concat_axis=2, tiled=True)
    return lax.all_to_all(slots, ("energy", "mom"), split_axis=2, concat_axis=2, tiled=True)


def rows_phase(received, row_ids, weights, deform_potential, reach):
    n_energy = lax.axis_size("energy")
    n_mom = lax.axis_size("mom")
    e_local = received.shape[1]
    span = received.shape[3]
    width = received.shape[4]
    total_rows = deform_potential.shape[0]
    grid = received.reshape(2, e_local, n_energy, n_mom, span * width)
    padded = jnp.pad(grid, ((0, 0), (0, 0), (1, 1), (0, 0), (0, 0)))
    total = None
    for index in range(weights.shape[0]):
        window = shifted_grid(grid, padded, index - reach)
        term = jnp.einsum("kq,zlaqx->zlakx", weights[index], window, precision=HIGH)
        total = term if total is None else total + term
    safe_rows = jnp.minimum(row_ids, total_rows - 1)
    row_scale = jnp.take(deform_potential, safe_rows)
    col_ids = (
        jnp.minimum(row_ids // width * width, total_rows - width)[:, None]
        + jnp.arange(width, dtype=jnp.int32)[None, :]
    )
    col_scale = jnp.take(deform_potential, col_ids)
    scale = (row_scale[:, None] * col_scale).reshape(span * width)
    sigma_rows = (total * scale).astype(jnp.bfloat16)
    diag_mask = jnp.arange(width, dtype=jnp.int32)[None, :] == (row_ids % width)[:, None]
    imag_part = grid[1].reshape(e_local, n_energy, n_mom, span, width)
    values = -jnp.sum(
        jnp.where(diag_mask[None, None, None], imag_part.astype(jnp.float32), 0.0),
        axis=(0, 1, 2, 4),
    )
    back = sigma_rows.reshape(2, e_local, n_energy * n_mom, span, width)
    return (back, values)


def body(
    inverse_blocks,
    coupling_blocks,
    shifts,
    emission_weight,
    absorption_weight,
    deform_potential,
    range_rows,
):
    green = solve_chain(inverse_blocks, coupling_blocks)
    e_local = green.shape[1]
    total_rows = green.shape[2]
    width = green.shape[3]
    devices = range_rows.shape[0]
    reach = SMAX
    weights = fold_weights(shifts, emission_weight, absorption_weight, reach)
    starts = jnp.cumsum(range_rows) - range_rows
    device = lax.axis_index(("energy", "mom"))
    span = 2 * total_rows // devices
    padded_green = jnp.pad(green, ((0, 0), (0, 0), (0, span), (0, 0)))
    slots = jax.vmap(
        lambda first: lax.dynamic_slice_in_dim(padded_green, first, span, 2), out_axes=2
    )(starts)
    received = relayout(slots, True)
    row_ids = starts[device] + jnp.arange(span, dtype=jnp.int32)
    back, values = rows_phase(received, row_ids, weights, deform_potential, reach)
    valid = jnp.arange(span, dtype=jnp.int32) < range_rows[device]
    charge = jnp.sum(jnp.where(valid, values, 0.0)).reshape(1)
    returned = relayout(back, False)
    all_rows = jnp.arange(total_rows, dtype=jnp.int32)
    owner = jnp.sum((all_rows[:, None] >= starts[None, :]).astype(jnp.int32), axis=1) - 1
    offset = all_rows - jnp.take(starts, owner)
    flat = returned.reshape(2, e_local, devices * span, width)
    sigma = jnp.take(flat, owner * span + offset, axis=2)[:, :, None]
    return (sigma, charge)


def solution(mesh):
    in_specs = (
        P(None, "energy", "mom", None, None),
        P(None, "mom", None, None),
        P(),
        P(),
        P(),
        P(),
        P(),
    )
    out_specs = (P(None, "energy", "mom", None, None), P(("energy", "mom")))
    return jax.shard_map(body, mesh=mesh, in_specs=in_specs, out_specs=out_specs, check_vma=False)
```

profile of v0, /device:TPU:1, one launch (start us, length us, event | category | flops | bytes accessed | tf_op | source)
XLA Modules:
  0.0 502.5 jit_solution(6645324879444803697)
XLA Ops:
  47.2 1.5 fusion.83
  48.7 1.5 fusion.98
  52.5 16.6 %copy.546 = bf16[2,2,2048,256]{3,1,0,2:T(2,128)(2,1)S(1)} copy(bf16[2,2,2048,256]{3,2,1,0:T(8,128)(2,1)S(1)} %bitcast.768) | data formatting | bytes 8388608 | tf_op jit(solution)/shard_map/reshape | solution.py:52
  69.1 5.7 %pad.8 = bf16[2,2,2080,256]{3,1,0,2:T(2,128)(2,1)} pad(bf16[2,2,2048,256]{3,1,0,2:T(2,128)(2,1)S(1)} %copy.546, bf16[]{:T(256)} %constant.106.clone.1), padding=0_0x0_0x0_32x0_0 | pad | bytes 8454146 | tf_op jit(solution)/shard_map/jit(_pad)/pad | solution.py:139
  74.7 23.3 %gather_fusion.1 = bf16[128,2,2,32,256]{4,2,1,3,0:T(2,128)(2,1)} fusion(bf16[2,2,2080,256]{3,1,0,2:T(2,128)(2,1)} %pad.8, s32[128]{0:T(128)S(1)} %get-tuple-element.8), kind=kCustom, calls=%fused_computation.1 | custom fusion | bytes 16779264 | tf_op jit(solution)/shard_map/vmap()/gather | solution.py:141
  98.0 12.0 %all-to-all-start = ((bf16[2,2,128,32,256]{4,1,0,3,2:T(2,128)(2,1)}), bf16[2,2,128,32,256]{4,1,0,3,2:T(2,128)(2,1)}, u32[]{:S(2)}, u32[]{:S(2)}) async-start(bf16[2,2,128,32,256]{4,1,0,3,2:T(2,128)(2,1)} %bitcast.706), calls=%async_computation | async-start | bytes 16777216 | tf_op jit(solution)/shard_map/all_to_all | solution.py:83
  113.5 45.5 %gather_fusion.3 = f32[8192]{0:T(1024)S(1)} fusion(f32[2048]{0:T(1024)S(1)} %copy-done, s32[8192]{0:T(1024)S(1)} %broadcast_clamp_fusion), kind=kCustom, calls=%fused_computation.3 | custom fusion | bytes 98304 | tf_op jit(solution)/shard_map/jit(_take)/gather | solution.py:107
  160.0 54.7 %all-to-all-done = bf16[2,2,128,32,256]{4,1,0,3,2:T(2,128)(2,1)} async-done(((bf16[2,2,128,32,256]{4,1,0,3,2:T(2,128)(2,1)}), bf16[2,2,128,32,256]{4,1,0,3,2:T(2,128)(2,1)}, u32[]{:S(2)}, u32[]{:S(2)}) %all-to-all-start) | async-done | bytes 8388640 | tf_op jit(solution)/shard_map/all_to_all | solution.py:83
  214.7 8.2 %copy.547 = bf16[2,2,128,32,256]{4,3,2,1,0:T(8,128)(2,1)} copy(bf16[2,2,128,32,256]{4,1,0,3,2:T(2,128)(2,1)} %all-to-all-done) | data formatting | bytes 16777216 | tf_op jit(solution)/shard_map/all_to_all | solution.py:83
  222.9 14.5 %reshape.298 = bf16[2,2,32,4,8192]{4,3,2,1,0:T(4,128)(2,1)} reshape(bf16[2,2,128,32,256]{4,3,2,1,0:T(8,128)(2,1)} %copy.547) | data formatting | bytes 16777216 | tf_op jit(solution)/shard_map/reshape | solution.py:94
  237.4 15.9 %fusion.292 = (bf16[2,1,32,4,8192]{4,3,2,1,0:T(4,128)(2,1)S(1)}, bf16[2,1,32,4,8192]{4,3,2,1,0:T(4,128)(2,1)}, bf16[2,1,32,4,8192]{4,3,2,1,0:T(4,128)(2,1)}, bf16[2,1,32,4,8192]{4,3,2,1,0:T(4,128)(2,1)}) fusion(bf16[2,2,32,4,8192]{4,3,2,1,0:T(4,128)(2,1)} %reshape.298), kind=kLoop, calls=%fused_computation.436 | loop fusion | bytes 33554432 | tf_op jit(solution)/shard_map/slice | solution.py:72
  253.3 17.4 %fusion.256 = f32[2,2,32,8192,4]{3,4,2,1,0:T(4,128)} fusion(bf16[2,2,32,4,8192]{4,3,2,1,0:T(4,128)(2,1)S(1)} %copy-done.2, f32[4,4]{1,0:T(4,128)S(1)} %bitcast.794, f32[4,4]{1,0:T(4,128)S(1)} %bitcast.795), kind=kOutput, calls=%fused_computation.391 | convolution fusion | flops 201326608 | bytes 25165952 | tf_op jit(solution)/shard_map/kq,zlaqx->zlakx/dot_general | solution.py:99
  270.7 18.7 %fusion.1 = f32[2,2,32,8192,4]{3,4,2,1,0:T(4,128)} fusion(bf16[2,1,32,4,8192]{4,3,2,1,0:T(4,128)(2,1)} %get-tuple-element.12, bf16[2,1,32,4,8192]{4,3,2,1,0:T(4,128)(2,1)} %get-tuple-element.13, f32[4,4]{1,0:T(4,128)S(1)} %bitcast.799, f32[4,4]{1,0:T(4,128)S(1)} %bitcast.800), kind=kOutput, calls=%fused_computation.7 | convolution fusion | flops 218103824 | bytes 25165952 | tf_op jit(solution)/shard_map/kq,zlaqx->zlakx/dot_general | solution.py:99
  289.4 26.9 %fusion = bf16[2,2,32,4,8192]{4,3,2,1,0:T(4,128)(2,1)} fusion(f32[2,2,32,8192,4]{3,4,2,1,0:T(4,128)} %fusion.1, f32[2,2,32,8192,4]{3,4,2,1,0:T(4,128)} %fusion.256, bf16[2,1,32,4,8192]{4,3,2,1,0:T(4,128)(2,1)S(1)} %copy-done.7, bf16[2,1,32,4,8192]{4,3,2,1,0:T(4,128)(2,1)S(1)} %get-tuple-element.10, f32[8192]{0:T(1024)S(1)} %select_multiply_fusion, ...), kind=kOutput, calls=%fused_computation.6 | convolution fusion | flops 234881040 | bytes 50364544 | tf_op jit(solution)/shard_map/kq,zlaqx->zlakx/dot_general | solution.py:99
  316.3 14.3 %reshape.299 = bf16[2,2,128,32,256]{4,3,2,1,0:T(8,128)(2,1)} reshape(bf16[2,2,32,4,8192]{4,3,2,1,0:T(4,128)(2,1)} %fusion) | data formatting | bytes 16777216 | tf_op jit(solution)/shard_map/reshape | solution.py:116
  330.6 8.1 %copy.548 = bf16[2,2,128,32,256]{4,3,1,0,2:T(8,128)(2,1)} copy(bf16[2,2,128,32,256]{4,3,2,1,0:T(8,128)(2,1)} %reshape.299) | data formatting | bytes 16777216 | tf_op jit(solution)/shard_map/reshape | solution.py:116
  338.6 5.7 %all-to-all-start.1 = ((bf16[2,2,128,32,256]{4,3,1,0,2:T(8,128)(2,1)}), bf16[2,2,128,32,256]{4,3,1,0,2:T(8,128)(2,1)}, u32[]{:S(2)}, u32[]{:S(2)}) async-start(bf16[2,2,128,32,256]{4,3,1,0,2:T(8,128)(2,1)} %copy.548), calls=%async_computation.1 | async-start | bytes 16777216 | tf_op jit(solution)/shard_map/all_to_all | solution.py:84
  345.3 12.6 %gather_fusion = s32[2048]{0:T(1024)S(1)} fusion(s32[128]{0:T(128)S(1)} %get-tuple-element.9, s32[2048]{0:T(1024)S(1)} %broadcast_clamp_fusion.2), kind=kCustom, calls=%fused_computation | custom fusion | bytes 24576 | tf_op jit(solution)/shard_map/jit(_take)/gather | solution.py:151
  358.7 6.8 %select_reduce_fusion = f32[32]{0:T(128)S(1)} fusion(pred[32,256]{1,0:T(8,128)(4,1)S(1)} %iota_compare_fusion.1, bf16[2,2,128,32,256]{4,1,0,3,2:T(2,128)(2,1)} %all-to-all-done), kind=kLoop, calls=%fused_computation.14 | loop fusion | flops 6291424 | bytes 4202624 | tf_op jit(solution)/shard_map/reduce_sum | solution.py:112
  366.7 82.5 %all-to-all-done.1 = bf16[2,2,128,32,256]{4,3,1,0,2:T(8,128)(2,1)} async-done(((bf16[2,2,128,32,256]{4,3,1,0,2:T(8,128)(2,1)}), bf16[2,2,128,32,256]{4,3,1,0,2:T(8,128)(2,1)}, u32[]{:S(2)}, u32[]{:S(2)}) %all-to-all-start.1) | async-done | bytes 8388640 | tf_op jit(solution)/shard_map/all_to_all | solution.py:84
  449.2 16.5 %copy.549 = bf16[2,2,128,32,256]{4,1,3,2,0:T(2,128)(2,1)} copy(bf16[2,2,128,32,256]{4,3,1,0,2:T(8,128)(2,1)} %all-to-all-done.1) | data formatting | bytes 16777216 | tf_op jit(solution)/shard_map/all_to_all | solution.py:84
  465.6 25.4 %gather_fusion.4 = bf16[2048,2,2,256]{3,2,1,0:T(2,128)(2,1)} fusion(bf16[2,2,4096,256]{3,1,2,0:T(2,128)(2,1)} %bitcast.767, s32[2048]{0:T(1024)S(1)} %broadcast_clamp_fusion.1), kind=kCustom, calls=%fused_computation.4 | custom fusion | bytes 8396800 | tf_op jit(solution)/shard_map/jit(_take)/gather | solution.py:153
  491.0 8.7 %broadcast_select_fusion = bf16[2,2,1,2048,256]{4,1,0,3,2:T(2,128)(2,1)S(1)} fusion(pred[2048]{0:T(1024)(128)(4,1)S(1)} %compare_and_fusion, bf16[2048,2,2,256]{3,2,1,0:T(2,128)(2,1)} %gather_fusion.4), kind=kLoop, calls=%fused_computation.15 | loop fusion | flops 2097152 | bytes 8390656 | tf_op jit(solution)/shard_map/jit(_take)/select_n | solution.py:153
  499.7 2.6 copy.550
  (198 shorter events, 55.6 us)
Async XLA Ops:
  0.6 110.6 %copy-start = (f32[2048]{0:T(1024)S(1)}, f32[2048]{0:T(1024)}, u32[]{:S(2)}) copy-start(f32[2048]{0:T(1024)} %param.12) | copy-start | bytes 24580
  5.7 6.5 %copy-start.3 = (bf16[2,2,1,2048,256]{4,3,2,1,0:T(8,128)(2,1)S(1)}, bf16[2,2,1,2048,256]{4,3,2,1,0:T(8,128)(2,1)}, u32[]{:S(2)}) copy-start(bf16[2,2,1,2048,256]{4,3,2,1,0:T(8,128)(2,1)} %param.7) | copy-start | bytes 12582916
  7.0 5.9 %copy-start.4 = (bf16[2,1,2048,256]{3,2,1,0:T(8,128)(2,1)S(1)}, bf16[2,1,2048,256]{3,2,1,0:T(8,128)(2,1)}, u32[]{:S(2)}) copy-start(bf16[2,1,2048,256]{3,2,1,0:T(8,128)(2,1)} %param.8) | copy-start | bytes 6291460
  40.1 2.5 copy-start.5
  41.7 4.4 copy-start.12
  42.3 3.8 copy-start.8
  48.7 3.3 copy-start.6
  98.0 116.7 %all-to-all-start = ((bf16[2,2,128,32,256]{4,1,0,3,2:T(2,128)(2,1)}), bf16[2,2,128,32,256]{4,1,0,3,2:T(2,128)(2,1)}, u32[]{:S(2)}, u32[]{:S(2)}) async-start(bf16[2,2,128,32,256]{4,1,0,3,2:T(2,128)(2,1)} %bitcast.706), calls=%async_computation | async-start | bytes 16777216 | tf_op jit(solution)/shard_map/all_to_all | solution.py:83
  113.5 45.7 %copy-start.9 = (f32[4,4,4]{2,1,0:T(4,128)S(1)}, f32[4,4,4]{2,1,0:T(4,128)}, u32[]{:S(2)}) copy-start(f32[4,4,4]{2,1,0:T(4,128)} %param.10) | copy-start | bytes 772
  113.5 45.7 %copy-start.11 = (s32[4]{0:T(128)S(1)}, s32[4]{0:T(128)}, u32[]{:S(2)}) copy-start(s32[4]{0:T(128)} %param.9) | copy-start | bytes 52
  113.5 46.1 %copy-start.10 = (f32[4,4,4]{2,1,0:T(4,128)S(1)}, f32[4,4,4]{2,1,0:T(4,128)}, u32[]{:S(2)}) copy-start(f32[4,4,4]{2,1,0:T(4,128)} %param.11) | copy-start | bytes 772
  237.4 15.9 %copy-start.2 = (bf16[2,2,32,4,8192]{4,3,2,1,0:T(4,128)(2,1)S(1)}, bf16[2,2,32,4,8192]{4,3,2,1,0:T(4,128)(2,1)}, u32[]{:S(2)}) copy-start(bf16[2,2,32,4,8192]{4,3,2,1,0:T(4,128)(2,1)} %reshape.298) | copy-start | bytes 25165828
  270.7 18.7 %copy-start.7 = (bf16[2,1,32,4,8192]{4,3,2,1,0:T(4,128)(2,1)S(1)}, bf16[2,1,32,4,8192]{4,3,2,1,0:T(4,128)(2,1)}, u32[]{:S(2)}) copy-start(bf16[2,1,32,4,8192]{4,3,2,1,0:T(4,128)(2,1)} %get-tuple-element.11) | copy-start | bytes 12582916
  338.6 5.7 %copy-start.13 = (s32[128]{0:T(128)S(1)}, s32[128]{0:T(128)}, u32[]{:S(2)}) copy-start(s32[128]{0:T(128)} %param.13) | copy-start | bytes 1540
  338.6 110.6 %all-to-all-start.1 = ((bf16[2,2,128,32,256]{4,3,1,0,2:T(8,128)(2,1)}), bf16[2,2,128,32,256]{4,3,1,0,2:T(8,128)(2,1)}, u32[]{:S(2)}, u32[]{:S(2)}) async-start(bf16[2,2,128,32,256]{4,3,1,0,2:T(8,128)(2,1)} %copy.548), calls=%async_computation.1 | async-start | bytes 16777216 | tf_op jit(solution)/shard_map/all_to_all | solution.py:84
  491.0 11.3 %copy-start.1 = (f32[2048]{0:T(1024)S(1)}, f32[2048]{0:T(1024)}, u32[]{:S(2)}) copy-start(f32[2048]{0:T(1024)} %param.12) | copy-start | bytes 24580
where the time goes:
time: 512 us; the launch traced here: 502 us
  local copies, waits for them, and re-layouts  212 us (41%)
  waiting for transfers between devices  137 us (27%)
  matrix products  113 us (22%)
  other arithmetic  21.2 us (4%)
  starting transfers between devices  17.6 us (3%)
    all_to_all x2, waiting for transfers between devices, relayout(): lax.all_to_all(slots, ('energy', 'mom'), split_axis=2, concat_axis=2, til...  137 us
    dot_general x3, matrix products, rows_phase(): term = jnp.einsum('kq,zlaqx->zlakx', weights[index], window, precision=HIGH)  63 us
    dot_general x124, matrix products, product(): return jnp.einsum(spec, first, second, preferred_element_type=jnp.float32)  49.2 us
    gather x1, local copies, waits for them, and re-layouts, rows_phase(): col_scale = jnp.take(deform_potential, col_ids)  45.5 us
    gather x1, local copies, waits for them, and re-layouts, body(): sigma = jnp.take(flat, owner * span + offset, axis=2)[:, :, None]  25.4 us
    all_to_all x2, local copies, waits for them, and re-layouts, relayout(): lax.all_to_all(slots, ('energy', 'mom'), split_axis=2, concat_axis=2, til...  24.6 us
    gather x1, local copies, waits for them, and re-layouts, body(): lax.dynamic_slice_in_dim(padded_green, first, span, 2)  23.3 us
    reshape x2, local copies, waits for them, and re-layouts, rows_phase(): back = sigma_rows.reshape(2, e_local, n_energy * n_mom, span, width)  22.4 us
  transfers between devices with their start and end apart: 2, of which 2 were waited for; matrix products, arithmetic and copies ran while one was open for 14% of the time, Pallas kernels for 0%

commit v1 on v0

v1 whole, which is shorter than its diff:
```python
import jax
import jax.numpy as jnp
from jax import lax
from jax.experimental import pallas as pl
from jax.experimental.pallas import tpu as pltpu
from jax.sharding import PartitionSpec as P

MESH = pl.DeviceIdType.MESH
F32 = jnp.float32
BF16 = jnp.bfloat16
B = 256
NB = 8
EL = 2
K = 4
Q = B // K
NE = 32
NT = (((1,), (1,)), ((), ()))


def mm(left, right):
    return jnp.dot(left, right, preferred_element_type=F32)


def mm_nt(left, right):
    return lax.dot_general(left, right, NT, preferred_element_type=F32)


def kernel(a_hbm, t_hbm, d_hbm, shifts, emission, absorption, range_rows, sigma, charge,
           av, tv, dv, gb, rb, hlo, hhi, sb, lmat, dens, dsum, dpart,
           a_sem, t_sem, d_sem, gs_sem, gr_sem, hs_sem, hr_sem, ss_sem, sr_sem, own_sem, ds_sem, dr_sem):
    E = lax.axis_index("energy")
    me = lax.axis_index("mom")
    x, rest = E // 8, lax.rem(E, 8)
    z, core = rest // 2, lax.rem(rest, 2)

    def mom_peer(d):
        return (E, lax.rem(me + d, K))

    def z_peer(d):
        return (x * 8 + lax.rem(z + d, 4) * 2 + core, me)

    def x_peer(d):
        return (lax.rem(E + 8 * d, NE), me)

    above, below = (lax.rem(E + 1, NE), me), (lax.rem(E + NE - 1, NE), me)
    twin = (x * 8 + z * 2 + 1 - core, me)
    greeted = [mom_peer(d) for d in (1, 2, 3)] + [above, below, twin]
    greeted += [z_peer(d) for d in (1, 2, 3)] + [x_peer(d) for d in (1, 2, 3)]

    barrier = pltpu.get_barrier_semaphore()
    for peer in greeted:
        pl.semaphore_signal(barrier, inc=1, device_id=peer, device_id_type=MESH)

    def t_copy(i):
        return pltpu.make_async_copy(t_hbm.at[:, 0, pl.ds(i * B, B), :], tv.at[i], t_sem.at[i])

    def a_copy(i):
        return pltpu.make_async_copy(a_hbm.at[:, :, 0, pl.ds(i * B, B), :], av.at[i], a_sem.at[i])

    def d_copy(i):
        return pltpu.make_async_copy(d_hbm.at[pl.ds(i * B, B)], dv.at[i], d_sem.at[i])

    for i in range(NB):
        t_copy(i).start()
        a_copy(i).start()
    for i in range(NB):
        d_copy(i).start()

    def gather(i, d):
        return pltpu.make_async_remote_copy(
            gb.at[i, lax.rem(me + d, K)], rb.at[i, :, me], gs_sem.at[i, d - 1], gr_sem.at[i, d - 1],
            device_id=mom_peer(d), device_id_type=MESH)

    def gathered(i, d):
        source = lax.rem(me + K - d, K)
        return pltpu.make_async_remote_copy(
            gb.at[i, source], rb.at[i, :, source], gs_sem.at[i, d - 1], gr_sem.at[i, d - 1],
            device_id=mom_peer(d), device_id_type=MESH)

    def halo_up(i):
        return pltpu.make_async_remote_copy(
            rb.at[i, 1], hlo.at[i], hs_sem.at[i, 0], hr_sem.at[i, 0], device_id=above, device_id_type=MESH)

    def halo_down(i):
        return pltpu.make_async_remote_copy(
            rb.at[i, 0], hhi.at[i], hs_sem.at[i, 1], hr_sem.at[i, 1], device_id=below, device_id_type=MESH)

    def scatter(i, d):
        return pltpu.make_async_remote_copy(
            sb.at[i, lax.rem(me + d, K)], sigma.at[:, :, 0, pl.ds(i * B + me * Q, Q), :],
            ss_sem.at[i, d - 1], sr_sem.at[i, d - 1], device_id=mom_peer(d), device_id_type=MESH)

    def scattered(i, d):
        source = lax.rem(me + K - d, K)
        return pltpu.make_async_remote_copy(
            sb.at[i, source], sigma.at[:, :, 0, pl.ds(i * B + source * Q, Q), :],
            ss_sem.at[i, d - 1], sr_sem.at[i, d - 1], device_id=mom_peer(d), device_id_type=MESH)

    def own_copy(i):
        return pltpu.make_async_copy(
            sb.at[i, me], sigma.at[:, :, 0, pl.ds(i * B + me * Q, Q), :], own_sem.at[i])

    picked = [(shifts[p] == 1).astype(F32) for p in range(4)]
    not_first = (E > 0).astype(F32)
    not_last = (E < NE - 1).astype(F32)
    weight = {}
    for k in range(K):
        for q in range(K):
            low, mid, high = 0.0, 0.0, 0.0
            for p in range(4):
                em, ab = emission[p, k, q], absorption[p, k, q]
                low = low + picked[p] * em
                high = high + picked[p] * ab
                mid = mid + (1.0 - picked[p]) * (em + ab)
            weight[k, q] = (low, mid, high)
    row = lax.broadcasted_iota(jnp.int32, (16, B), 0)
    col = lax.broadcasted_iota(jnp.int32, (16, B), 1)
    group, same = col // 16, lax.rem(col, 16) == row
    for e in range(EL):
        for k in range(K):
            tile = jnp.zeros((16, B), F32)
            for part in range(3):
                source = e + part
                for q in range(K):
                    value = weight[k, q][part]
                    if source == 0:
                        value = value * not_first
                    if source == 3:
                        value = value * not_last
                    tile = jnp.where(group == source * K + q, value, tile)
            tile = jnp.where(same, tile, 0.0)
            top = tile.astype(BF16)
            at = (e * K + k) * 16
            lmat[at:at + 16, :] = top
            lmat[128 + at:128 + at + 16, :] = (tile - top.astype(F32)).astype(BF16)

    eye = lax.broadcasted_iota(jnp.int32, (B, B), 0) == lax.broadcasted_iota(jnp.int32, (B, B), 1)

    def rows_of(i, e, c):
        return gb[i, :, e, c].reshape(B, B)

    def solve(i, first):
        t_copy(i).wait()
        t_re, t_im = tv[i, 0], tv[i, 1]
        t_cat = jnp.concatenate([t_re, t_im], axis=1)
        t_swap = jnp.concatenate([-t_im, t_re], axis=1)
        if first:
            left = t_cat
        else:
            parts = []
            for e in range(EL):
                g_re, g_im = rows_of(i - 1, e, 0), rows_of(i - 1, e, 1)
                p_re = mm(t_cat, jnp.concatenate([g_re, -g_im], axis=0)).astype(BF16)
                p_im = mm(t_cat, jnp.concatenate([g_im, g_re], axis=0)).astype(BF16)
                parts.append(jnp.concatenate([p_re, p_im], axis=1))
            left = jnp.concatenate(parts, axis=0)
        s_re = mm_nt(left, t_cat).astype(BF16)
        s_im = mm_nt(left, t_swap).astype(BF16)
        a_copy(i).wait()
        trace = None
        for e in range(EL):
            at = 0 if first else e * B
            a_re, a_im = av[i, 0, e], av[i, 1, e]
            c_re, c_im = s_re[at:at + B], s_im[at:at + B]
            a_cat = jnp.concatenate([a_re, a_im], axis=1)
            q_re = mm(a_cat, jnp.concatenate([c_re, -c_im], axis=0)).astype(BF16)
            q_im = mm(a_cat, jnp.concatenate([c_im, c_re], axis=0)).astype(BF16)
            q_cat = jnp.concatenate([q_re, q_im], axis=1)
            h_re = mm(q_cat, jnp.concatenate([a_re, -a_im], axis=0))
            h_im = mm(q_cat, jnp.concatenate([a_im, a_re], axis=0))
            g_re = (a_re.astype(F32) + h_re).astype(BF16)
            g_im = (a_im.astype(F32) + h_im).astype(BF16)
            gb[i, :, e, 0] = g_re.reshape(K, Q, B)
            gb[i, :, e, 1] = g_im.reshape(K, Q, B)
            wide = g_im.astype(F32)
            trace = wide if trace is None else trace + wide
        dens[pl.ds(i, 1), :] = -jnp.sum(jnp.where(eye, trace, 0.0), axis=0, keepdims=True)

    def ship(i):
        for d in (1, 3, 2):
            gather(i, d).start()
        rb[i, :, me] = gb[i, me]

    solve(0, True)
    pl.semaphore_wait(barrier, len(greeted))
    ship(0)

    def chain(i, carry):
        solve(i, False)
        ship(i)
        return carry

    lax.fori_loop(1, NB, chain, 0)

    stages = [[mom_peer(d) for d in (1, 2, 3)], [twin], [z_peer(d) for d in (1, 2, 3)], [x_peer(d) for d in (1, 2, 3)]]

    def density_copy(stage, n):
        source = dens if stage == 0 else dsum.at[stage - 1]
        return pltpu.make_async_remote_copy(
            source, dpart.at[stage, n], ds_sem.at[stage, n], dr_sem.at[stage, n],
            device_id=stages[stage][n], device_id_type=MESH)

    def density_send(stage):
        for n in range(len(stages[stage])):
            density_copy(stage, n).start()

    def density_add(stage):
        total = dens[...] if stage == 0 else dsum[stage - 1]
        for n in range(len(stages[stage])):
            density_copy(stage, n).wait_recv()
            total = total + dpart[stage, n]
        dsum[stage] = total

    density_send(0)
    for i in range(NB):
        d_copy(i).wait()

    def mix(i):
        d_row = dv[pl.ds(i, 1), :]
        hit = (lax.broadcasted_iota(jnp.int32, (Q, B), 1)
               == lax.broadcasted_iota(jnp.int32, (Q, B), 0) + me * Q)
        d_col = jnp.sum(jnp.where(hit, d_row, 0.0), axis=1, keepdims=True)
        scale = d_col * d_row
        for c in range(2):
            for r in range(0, Q, 16):
                parts = [hlo[i, q, c, r:r + 16] for q in range(K)]
                for e in range(EL):
                    parts += [rb[i, e, q, c, r:r + 16] for q in range(K)]
                parts += [hhi[i, q, c, r:r + 16] for q in range(K)]
                out = mm(lmat[...], jnp.concatenate(parts, axis=0))
                out = (out[:128] + out[128:]).reshape(EL, K, 16, B) * scale[r:r + 16][None, None]
                out = out.astype(BF16)
                for e in range(EL):
                    for k in range(K):
                        sb[i, k, c, e, r:r + 16] = out[e, k]

    def step(i, carry):
        @pl.when(i < NB)
        def _():
            for d in (1, 2, 3):
                gathered(i, d).wait_recv()
            halo_up(i).start()
            halo_down(i).start()

        for stage in range(4):
            @pl.when(i == 2 + stage)
            def _(stage=stage):
                density_add(stage)
                if stage < 3:
                    density_send(stage + 1)

        @pl.when(i > 0)
        def _():
            halo_up(i - 1).wait_recv()
            halo_down(i - 1).wait_recv()
            mix(i - 1)
            for d in (1, 3, 2):
                scatter(i - 1, d).start()
            own_copy(i - 1).start()
        return carry

    lax.fori_loop(0, NB + 1, step, 0)

    device = E * K + me
    start = 0
    for n in range(NE * K):
        start = start + jnp.where(n < device, range_rows[n], 0)
    stop = start + range_rows[device]
    row_id = lax.broadcasted_iota(jnp.int32, (NB, B), 0) * B + lax.broadcasted_iota(jnp.int32, (NB, B), 1)
    inside = (row_id >= start) & (row_id < stop)
    charge[0] = jnp.sum(jnp.where(inside, dsum[3], 0.0))

    def finish(i, carry):
        for d in (1, 2, 3):
            gather(i, d).wait_send()
            scatter(i, d).wait_send()
            scattered(i, d).wait_recv()
        halo_up(i).wait_send()
        halo_down(i).wait_send()
        own_copy(i).wait()
        return carry

    lax.fori_loop(0, NB, finish, 0)
    for stage in range(4):
        for n in range(len(stages[stage])):
            density_copy(stage, n).wait_send()


def body(inverse_blocks, coupling_blocks, shifts, emission_weight, absorption_weight, deform_potential, range_rows):
    smem = pl.BlockSpec(memory_space=pltpu.SMEM)
    hbm = pl.BlockSpec(memory_space=pl.ANY)
    dma = pltpu.SemaphoreType.DMA
    return pl.pallas_call(
        kernel,
        out_shape=(
            jax.ShapeDtypeStruct(inverse_blocks.shape, BF16),
            jax.ShapeDtypeStruct((1,), F32),
        ),
        in_specs=[hbm, hbm, hbm, smem, smem, smem, smem],
        out_specs=(hbm, smem),
        scratch_shapes=[
            pltpu.VMEM((NB, 2, EL, B, B), BF16),
            pltpu.VMEM((NB, 2, B, B), BF16),
            pltpu.VMEM((NB, B), F32),
            pltpu.VMEM((NB, K, EL, 2, Q, B), BF16),
            pltpu.VMEM((NB, EL, K, 2, Q, B), BF16),
            pltpu.VMEM((NB, K, 2, Q, B), BF16),
            pltpu.VMEM((NB, K, 2, Q, B), BF16),
            pltpu.VMEM((NB, K, 2, EL, Q, B), BF16),
            pltpu.VMEM((B, B), BF16),
            pltpu.VMEM((NB, B), F32),
            pltpu.VMEM((4, NB, B), F32),
            pltpu.VMEM((4, 3, NB, B), F32),
            dma((NB,)), dma((NB,)), dma((NB,)),
            dma((NB, 3)), dma((NB, 3)),
            dma((NB, 2)), dma((NB, 2)),
            dma((NB, 3)), dma((NB, 3)),
            dma((NB,)),
            dma((4, 3)), dma((4, 3)),
        ],
        compiler_params=pltpu.CompilerParams(
            collective_id=0, has_side_effects=True, vmem_limit_bytes=48 << 20),
    )(inverse_blocks, coupling_blocks, deform_potential, shifts, emission_weight, absorption_weight, range_rows)


def solution(mesh):
    in_specs = (
        P(None, "energy", "mom", None, None),
        P(None, "mom", None, None),
        P(),
        P(),
        P(),
        P(),
        P(),
    )
    out_specs = (P(None, "energy", "mom", None, None), P(("energy", "mom")))
    return jax.shard_map(body, mesh=mesh, in_specs=in_specs, out_specs=out_specs, check_vma=False)
```

time: 512 us -> 114 us (0.22); the launches traced: 502 us -> 112 us
  local copies, waits for them, and re-layouts: 212 us -> 9.45 us
  waiting for transfers between devices: 137 us -> 0 us
  matrix products: 113 us -> 0 us
  Pallas kernels: 0 us -> 100 us
  other arithmetic: 21.2 us -> 0 us
  starting transfers between devices: 17.6 us -> 0 us
    all_to_all x2 -> x0, waiting for transfers between devices: 137 us -> none  [relayout(): lax.all_to_all(slots, ('energy', 'mom'), split_axis=2, concat_axis=2, til...]
    dot_general x133 -> x0, matrix products: 113 us -> none  [the longest x3 63 us: rows_phase(): term = jnp.einsum('kq,zlaqx->zlakx', weights[index], window, precision=HIGH)]
    gather x5 -> x0, local copies, waits for them, and re-layouts: 107 us -> none  [the longest x1 45.5 us: rows_phase(): col_scale = jnp.take(deform_potential, col_ids)]
    pallas_call x0 -> x1, Pallas kernels: none -> 100 us  [body(): pl.pallas_call(kernel, out_shape=(jax.ShapeDtypeStruct(inverse_blocks.sha...]
    reshape x4 -> x0, local copies, waits for them, and re-layouts: 53.5 us -> none  [the longest x2 22.4 us: rows_phase(): back = sigma_rows.reshape(2, e_local, n_energy * n_mom, span, width)]
    all_to_all x2 -> x0, local copies, waits for them, and re-layouts: 24.6 us -> none  [relayout(): lax.all_to_all(slots, ('energy', 'mom'), split_axis=2, concat_axis=2, til...]
    all_to_all x2 -> x0, starting transfers between devices: 17.6 us -> none  [relayout(): lax.all_to_all(slots, ('energy', 'mom'), split_axis=2, concat_axis=2, til...]
    slice x1 -> x0, local copies, waits for them, and re-layouts: 15.9 us -> none  [shifted_grid(): first = padded[:, offset:, 1:1 + n_energy]]
  transfers between devices with their start and end apart: 2 -> 0, of which waited for: 2 -> 0; matrix products, arithmetic and copies ran while one was open for 14% -> 0% of each run, Pallas kernels for 0% -> 0%
where the time goes in v1:
time: 114 us; the launch traced here: 112 us
  Pallas kernels  100 us (88%)
  local copies, waits for them, and re-layouts  9.45 us (8%)
  between operations  2.4 us (2%)
    pallas_call x1, Pallas kernels, body(): pl.pallas_call(kernel, out_shape=(jax.ShapeDtypeStruct(inverse_blocks.sha...  100 us
    unnamed x13, local copies, waits for them, and re-layouts  9.45 us

profile of v1, /device:TPU:1, one launch (start us, length us, event | category | flops | bytes accessed | tf_op | source)
XLA Modules:
  0.0 111.9 jit_solution(3653624905094433004)
XLA Ops:
  0.6 0.0 copy-start
  0.6 1.6 %copy-done = bf16[2,1,2048,256]{3,2,1,0:T(8,128)(2,1)S(1)} copy-done((bf16[2,1,2048,256]{3,2,1,0:T(8,128)(2,1)S(1)}, bf16[2,1,2048,256]{3,2,1,0:T(8,128)(2,1)}, u32[]{:S(2)}) %copy-start) | copy-done | bytes 2097176
  2.2 0.0 copy-start.1
  2.2 0.7 copy-done.1
  2.9 0.0 copy-start.2
  2.9 0.7 copy-done.2
  3.6 0.0 copy-start.3
  3.6 0.7 copy-done.3
  4.3 0.0 copy-start.4
  4.3 0.7 copy-done.4
  5.0 0.0 copy-start.5
  5.0 0.7 copy-done.5
  5.6 100.0 %shard_map.86 = (bf16[2,2,1,2048,256]{4,3,2,1,0:T(8,128)(2,1)}, f32[1]{0:T(128)}) custom-call(bf16[2,2,1,2048,256]{4,3,2,1,0:T(8,128)(2,1)} %a_hbm.1, bf16[2,1,2048,256]{3,2,1,0:T(8,128)(2,1)S(1)} %copy-done, f32[2048]{0:T(1024)S(1)} %copy-done.1, s32[4]{0:T(128)S(1)} %copy-done.4, f32[4,4,4]{2,1,0:T(4,128)S(1)} %copy-done.2, f32[4,4,4]{2,1,0:T(4,128)S(1)} %copy-done.3, ...), custom_call_target="tpu_custom_call" | custom-call | tf_op jit(solution)/shard_map/pallas_call | solution.py:293
  105.7 4.5 %copy.11 = bf16[2,2,1,2048,256]{4,3,2,1,0:T(8,128)(2,1)} copy(bf16[2,2,1,2048,256]{4,3,2,1,0:T(8,128)(2,1)} %get-tuple-element.4) | data formatting | bytes 8388608
Async XLA Ops:
  0.6 1.6 %copy-start = (bf16[2,1,2048,256]{3,2,1,0:T(8,128)(2,1)S(1)}, bf16[2,1,2048,256]{3,2,1,0:T(8,128)(2,1)}, u32[]{:S(2)}) copy-start(bf16[2,1,2048,256]{3,2,1,0:T(8,128)(2,1)} %t_hbm.1) | copy-start | bytes 6291460
  2.2 0.7 copy-start.1
  2.9 0.7 copy-start.2
  3.6 0.7 copy-start.3
  4.3 0.7 copy-start.4
  5.0 0.7 copy-start.5

commit v2 on v1

--- a/solution.py
+++ b/solution.py
@@ -25,8 +25,8 @@
     return lax.dot_general(left, right, NT, preferred_element_type=F32)
 
 
-def kernel(a_hbm, t_hbm, d_hbm, shifts, emission, absorption, range_rows, sigma, charge,
-           av, tv, dv, gb, rb, hlo, hhi, sb, lmat, dens, dsum, dpart,
+def kernel(a_hbm, t_hbm, d_hbm, shifts_hbm, emission_hbm, absorption_hbm, range_hbm, sigma, charge,
+           shifts, emission, absorption, range_rows, small_sem, av, tv, dv, gb, rb, hlo, hhi, sb, lmat, dens, dsum, dpart,
            a_sem, t_sem, d_sem, gs_sem, gr_sem, hs_sem, hr_sem, ss_sem, sr_sem, own_sem, ds_sem, dr_sem):
     E = lax.axis_index("energy")
     me = lax.axis_index("mom")
@@ -60,9 +60,13 @@
     def d_copy(i):
         return pltpu.make_async_copy(d_hbm.at[pl.ds(i * B, B)], dv.at[i], d_sem.at[i])
 
+    small = ((shifts_hbm, shifts), (emission_hbm, emission), (absorption_hbm, absorption), (range_hbm, range_rows))
     for i in range(NB):
         t_copy(i).start()
         a_copy(i).start()
+        if i == 0:
+            for n, (source, target) in enumerate(small):
+                pltpu.make_async_copy(source, target, small_sem.at[n]).start()
     for i in range(NB):
         d_copy(i).start()
 
@@ -99,40 +103,6 @@
     def own_copy(i):
         return pltpu.make_async_copy(
             sb.at[i, me], sigma.at[:, :, 0, pl.ds(i * B + me * Q, Q), :], own_sem.at[i])
-
-    picked = [(shifts[p] == 1).astype(F32) for p in range(4)]
-    not_first = (E > 0).astype(F32)
-    not_last = (E < NE - 1).astype(F32)
-    weight = {}
-    for k in range(K):
-        for q in range(K):
-            low, mid, high = 0.0, 0.0, 0.0
-            for p in range(4):
-                em, ab = emission[p, k, q], absorption[p, k, q]
-                low = low + picked[p] * em
-                high = high + picked[p] * ab
-                mid = mid + (1.0 - picked[p]) * (em + ab)
-            weight[k, q] = (low, mid, high)
-    row = lax.broadcasted_iota(jnp.int32, (16, B), 0)
-    col = lax.broadcasted_iota(jnp.int32, (16, B), 1)
-    group, same = col // 16, lax.rem(col, 16) == row
-    for e in range(EL):
-        for k in range(K):
-            tile = jnp.zeros((16, B), F32)
-            for part in range(3):
-                source = e + part
-                for q in range(K):
-                    value = weight[k, q][part]
-                    if source == 0:
-                        value = value * not_first
-                    if source == 3:
-                        value = value * not_last
-                    tile = jnp.where(group == source * K + q, value, tile)
-            tile = jnp.where(same, tile, 0.0)
-            top = tile.astype(BF16)
-            at = (e * K + k) * 16
-            lmat[at:at + 16, :] = top
-            lmat[128 + at:128 + at + 16, :] = (tile - top.astype(F32)).astype(BF16)
 
     eye = lax.broadcasted_iota(jnp.int32, (B, B), 0) == lax.broadcasted_iota(jnp.int32, (B, B), 1)
 
@@ -185,6 +155,42 @@
     pl.semaphore_wait(barrier, len(greeted))
     ship(0)
 
+    for n, (source, target) in enumerate(small):
+        pltpu.make_async_copy(source, target, small_sem.at[n]).wait()
+    picked = [(shifts[p] == 1).astype(F32) for p in range(4)]
+    not_first = (E > 0).astype(F32)
+    not_last = (E < NE - 1).astype(F32)
+    weight = {}
+    for k in range(K):
+        for q in range(K):
+            low, mid, high = 0.0, 0.0, 0.0
+            for p in range(4):
+                em, ab = emission[p, k, q], absorption[p, k, q]
+                low = low + picked[p] * em
+                high = high + picked[p] * ab
+                mid = mid + (1.0 - picked[p]) * (em + ab)
+            weight[k, q] = (low, mid, high)
+    row = lax.broadcasted_iota(jnp.int32, (16, B), 0)
+    col = lax.broadcasted_iota(jnp.int32, (16, B), 1)
+    group, same = col // 16, lax.rem(col, 16) == row
+    for e in range(EL):
+        for k in range(K):
+            tile = jnp.zeros((16, B), F32)
+            for part in range(3):
+                source = e + part
+                for q in range(K):
+                    value = weight[k, q][part]
+                    if source == 0:
+                        value = value * not_first
+                    if source == 3:
+                        value = value * not_last
+                    tile = jnp.where(group == source * K + q, value, tile)
+            tile = jnp.where(same, tile, 0.0)
+            top = tile.astype(BF16)
+            at = (e * K + k) * 16
+            lmat[at:at + 16, :] = top
+            lmat[128 + at:128 + at + 16, :] = (tile - top.astype(F32)).astype(BF16)
+
     def chain(i, carry):
         solve(i, False)
         ship(i)
@@ -288,7 +294,7 @@
 
 def body(inverse_blocks, coupling_blocks, shifts, emission_weight, absorption_weight, deform_potential, range_rows):
     smem = pl.BlockSpec(memory_space=pltpu.SMEM)
-    hbm = pl.BlockSpec(memory_space=pl.ANY)
+    hbm = pl.BlockSpec(memory_space=pltpu.HBM)
     dma = pltpu.SemaphoreType.DMA
     return pl.pallas_call(
         kernel,
@@ -296,9 +302,14 @@
             jax.ShapeDtypeStruct(inverse_blocks.shape, BF16),
             jax.ShapeDtypeStruct((1,), F32),
         ),
-        in_specs=[hbm, hbm, hbm, smem, smem, smem, smem],
+        in_specs=[hbm] * 7,
         out_specs=(hbm, smem),
         scratch_shapes=[
+            pltpu.SMEM((4,), jnp.int32),
+            pltpu.SMEM((4, K, K), F32),
+            pltpu.SMEM((4, K, K), F32),
+            pltpu.SMEM((NE * K,), jnp.int32),
+            dma((4,)),
             pltpu.VMEM((NB, 2, EL, B, B), BF16),
             pltpu.VMEM((NB, 2, B, B), BF16),
             pltpu.VMEM((NB, B), F32),
@@ -320,7 +331,7 @@
         ],
         compiler_params=pltpu.CompilerParams(
             collective_id=0, has_side_effects=True, vmem_limit_bytes=48 << 20),
-    )(inverse_blocks, coupling_blocks, deform_potential, shifts, emission_weight, absorption_weight, range_rows)
+    )(*[pltpu.with_memory_space_constraint(v, pltpu.HBM) for v in (inverse_blocks, coupling_blocks, deform_potential, shifts, emission_weight, absorption_weight, range_rows)])
 
 
 def solution(mesh):

time: 114 us -> 105 us (0.921)
  local copies, waits for them, and re-layouts: 9.45 us -> 2.02 us
    unnamed x13 -> x1, local copies, waits for them, and re-layouts: 9.45 us -> 2.02 us
where the time goes in v2:
time: 105 us; the launch traced here: 104 us
  Pallas kernels  99.2 us (94%)
  between operations  2.33 us (2%)
  local copies, waits for them, and re-layouts  2.02 us (2%)
    pallas_call x1, Pallas kernels, body(): pl.pallas_call(kernel, out_shape=(jax.ShapeDtypeStruct(inverse_blocks.sha...  99.2 us

profile of v2, /device:TPU:1, one launch (start us, length us, event | category | flops | bytes accessed | tf_op | source)
XLA Modules:
  0.0 103.6 jit_solution(8097742447975067729)
XLA Ops:
  0.6 99.2 %shard_map.86 = (bf16[2,2,1,2048,256]{4,3,2,1,0:T(8,128)(2,1)S(1)}, f32[1]{0:T(128)}) custom-call(bf16[2,2,1,2048,256]{4,3,2,1,0:T(8,128)(2,1)} %a_hbm.1, bf16[2,1,2048,256]{3,2,1,0:T(8,128)(2,1)} %t_hbm.1, f32[2048]{0:T(1024)} %d_hbm.1, s32[4]{0:T(128)} %shifts_hbm.1, f32[4,4,4]{2,1,0:T(4,128)} %emission_hbm.1, f32[4,4,4]{2,1,0:T(4,128)} %absorption_hbm.1, ...), custom_call_target="tpu_custom_call" | custom-call | tf_op jit(solution)/shard_map/pallas_call | solution.py:299
  99.8 2.0 %copy.11 = bf16[2,2,1,2048,256]{4,3,2,1,0:T(8,128)(2,1)} copy(bf16[2,2,1,2048,256]{4,3,2,1,0:T(8,128)(2,1)S(1)} %get-tuple-element.4) | data formatting | bytes 8388608

commit v3 on v2

--- a/solution.py
+++ b/solution.py
@@ -274,7 +274,7 @@
     stop = start + range_rows[device]
     row_id = lax.broadcasted_iota(jnp.int32, (NB, B), 0) * B + lax.broadcasted_iota(jnp.int32, (NB, B), 1)
     inside = (row_id >= start) & (row_id < stop)
-    charge[0] = jnp.sum(jnp.where(inside, dsum[3], 0.0))
+    charge[...] = jnp.full((1, 128), jnp.sum(jnp.where(inside, dsum[3], 0.0)), F32)
 
     def finish(i, carry):
         for d in (1, 2, 3):
@@ -292,18 +292,28 @@
             density_copy(stage, n).wait_send()
 
 
+def place(landed, total, sigma, charge, sems):
+    copies = [pltpu.make_async_copy(total, charge, sems.at[NB])]
+    for i in range(4):
+        copies.append(pltpu.make_async_copy(landed.at[i // 2, i % 2], sigma.at[i // 2, i % 2], sems.at[i]))
+    for copy in copies:
+        copy.start()
+    for copy in copies:
+        copy.wait()
+
+
 def body(inverse_blocks, coupling_blocks, shifts, emission_weight, absorption_weight, deform_potential, range_rows):
     smem = pl.BlockSpec(memory_space=pltpu.SMEM)
     hbm = pl.BlockSpec(memory_space=pltpu.HBM)
     dma = pltpu.SemaphoreType.DMA
-    return pl.pallas_call(
+    landed, total = pl.pallas_call(
         kernel,
         out_shape=(
             jax.ShapeDtypeStruct(inverse_blocks.shape, BF16),
-            jax.ShapeDtypeStruct((1,), F32),
+            jax.ShapeDtypeStruct((1, 128), F32),
         ),
         in_specs=[hbm] * 7,
-        out_specs=(hbm, smem),
+        out_specs=(hbm, pl.BlockSpec(memory_space=pltpu.VMEM)),
         scratch_shapes=[
             pltpu.SMEM((4,), jnp.int32),
             pltpu.SMEM((4, K, K), F32),
@@ -332,6 +342,17 @@
         compiler_params=pltpu.CompilerParams(
             collective_id=0, has_side_effects=True, vmem_limit_bytes=48 << 20),
     )(*[pltpu.with_memory_space_constraint(v, pltpu.HBM) for v in (inverse_blocks, coupling_blocks, deform_potential, shifts, emission_weight, absorption_weight, range_rows)])
+    return pl.pallas_call(
+        place,
+        out_shape=(
+            jax.ShapeDtypeStruct(landed.shape, BF16),
+            jax.ShapeDtypeStruct((1,), F32),
+        ),
+        in_specs=[pl.BlockSpec(memory_space=pl.ANY)] * 2,
+        out_specs=(hbm, hbm),
+        scratch_shapes=[dma((NB + 1,))],
+        compiler_params=pltpu.CompilerParams(vmem_limit_bytes=8 << 20),
+    )(landed, total[0, :1])
 
 
 def solution(mesh):

time: 105 us -> 103 us (0.981)
  local copies, waits for them, and re-layouts: 2.02 us -> 0 us
  Pallas kernels: 99.2 us -> 101 us
  between operations: 2.33 us -> 0.64 us
    pallas_call x0 -> x1, Pallas kernels: none -> 2.12 us  [body(): pl.pallas_call(place, out_shape=(jax.ShapeDtypeStruct(landed.shape, BF16)...]
    unnamed x1 -> x0, local copies, waits for them, and re-layouts: 2.02 us -> none
where the time goes in v3:
time: 103 us; the launch traced here: 101 us
  Pallas kernels  101 us (98%)
    pallas_call x1, Pallas kernels, body(): pl.pallas_call(kernel, out_shape=(jax.ShapeDtypeStruct(inverse_blocks.sha...  98.7 us
    pallas_call x1, Pallas kernels, body(): pl.pallas_call(place, out_shape=(jax.ShapeDtypeStruct(landed.shape, BF16)...  2.12 us

profile of v3, /device:TPU:1, one launch (start us, length us, event | category | flops | bytes accessed | tf_op | source)
XLA Modules:
  0.0 101.5 jit_solution(2356161049415486079)
XLA Ops:
  0.6 98.7 %shard_map.86 = (bf16[2,2,1,2048,256]{4,3,2,1,0:T(8,128)(2,1)S(1)}, f32[1,128]{1,0:T(1,128)S(1)}) custom-call(bf16[2,2,1,2048,256]{4,3,2,1,0:T(8,128)(2,1)} %a_hbm.1, bf16[2,1,2048,256]{3,2,1,0:T(8,128)(2,1)} %t_hbm.1, f32[2048]{0:T(1024)} %d_hbm.1, s32[4]{0:T(128)} %shifts_hbm.1, f32[4,4,4]{2,1,0:T(4,128)} %emission_hbm.1, f32[4,4,4]{2,1,0:T(4,128)} %absorption_hbm.1, ...), custom_call_target="tpu_custom_call" | custom-call | tf_op jit(solution)/shard_map/pallas_call | solution.py:309
  99.3 2.1 %shard_map.87 = (bf16[2,2,1,2048,256]{4,3,2,1,0:T(8,128)(2,1)}, f32[1]{0:T(128)}) custom-call(bf16[2,2,1,2048,256]{4,3,2,1,0:T(8,128)(2,1)S(1)} %get-tuple-element.4.landed, f32[1]{0:T(128)S(1)} %bitcast.2), custom_call_target="tpu_custom_call" | custom-call | tf_op jit(solution)/shard_map/pallas_call | solution.py:345

commit v4 on v3

--- a/solution.py
+++ b/solution.py
@@ -27,7 +27,7 @@
 
 def kernel(a_hbm, t_hbm, d_hbm, shifts_hbm, emission_hbm, absorption_hbm, range_hbm, sigma, charge,
            shifts, emission, absorption, range_rows, small_sem, av, tv, dv, gb, rb, hlo, hhi, sb, lmat, dens, dsum, dpart,
-           a_sem, t_sem, d_sem, gs_sem, gr_sem, hs_sem, hr_sem, ss_sem, sr_sem, own_sem, ds_sem, dr_sem):
+           a_sem, t_sem, d_sem, gs_sem, gr_sem, hs_sem, hr_sem, ss_sem, sr_sem, own_sem, ds_sem, dr_sem, told):
     E = lax.axis_index("energy")
     me = lax.axis_index("mom")
     x, rest = E // 8, lax.rem(E, 8)
@@ -44,12 +44,50 @@
 
     above, below = (lax.rem(E + 1, NE), me), (lax.rem(E + NE - 1, NE), me)
     twin = (x * 8 + z * 2 + 1 - core, me)
-    greeted = [mom_peer(d) for d in (1, 2, 3)] + [above, below, twin]
-    greeted += [z_peer(d) for d in (1, 2, 3)] + [x_peer(d) for d in (1, 2, 3)]
+    COUNTER, ENVOY = 1, 3
+    is_counter, is_envoy = (me == COUNTER) & (core == 1), (me == ENVOY) & (core == 1)
+    home = E - core
+    rings = [(x * 8 + lax.rem(z + d, 4) * 2) for d in (1, 2, 3)] + [lax.rem(home + 8 * d, NE) for d in (1, 2, 3)]
+    rings += [lax.rem(home + 2, NE), lax.rem(home + NE - 2, NE)]
 
     barrier = pltpu.get_barrier_semaphore()
-    for peer in greeted:
-        pl.semaphore_signal(barrier, inc=1, device_id=peer, device_id_type=MESH)
+    for d in (1, 2, 3):
+        @pl.when((core == 0) | (lax.rem(me + d, K) != ENVOY))
+        def _(d=d):
+            pl.semaphore_signal(barrier, inc=1, device_id=mom_peer(d), device_id_type=MESH)
+
+    @pl.when(core == 0)
+    def _():
+        pl.semaphore_signal(barrier, inc=1, device_id=(home + 1, COUNTER), device_id_type=MESH)
+
+    def ring_ready():
+        @pl.when(is_counter)
+        def _():
+            pl.semaphore_wait(barrier, 7)
+            pl.semaphore_signal(told, inc=1, device_id=(E, ENVOY), device_id_type=MESH)
+
+        @pl.when(is_envoy)
+        def _():
+            pl.semaphore_wait(told, 1)
+            for ring in rings:
+                pl.semaphore_signal(barrier, inc=1, device_id=(ring + 1, ENVOY), device_id_type=MESH)
+
+        @pl.when(jnp.logical_not(is_counter | is_envoy))
+        def _():
+            pl.semaphore_wait(barrier, 3)
+
+    def outside_ready():
+        @pl.when(is_envoy)
+        def _():
+            pl.semaphore_wait(barrier, len(rings))
+            for mom in range(K):
+                pl.semaphore_signal(told, inc=1, device_id=(home, mom), device_id_type=MESH)
+                if mom != ENVOY:
+                    pl.semaphore_signal(told, inc=1, device_id=(home + 1, mom), device_id_type=MESH)
+
+        @pl.when(jnp.logical_not(is_envoy))
+        def _():
+            pl.semaphore_wait(told, 1)
 
     def t_copy(i):
         return pltpu.make_async_copy(t_hbm.at[:, 0, pl.ds(i * B, B), :], tv.at[i], t_sem.at[i])
@@ -109,27 +147,49 @@
     def rows_of(i, e, c):
         return gb[i, :, e, c].reshape(B, B)
 
-    def solve(i, first):
+    def note(i):
+        wide = rows_of(i, 0, 1).astype(F32) + rows_of(i, 1, 1).astype(F32)
+        dens[pl.ds(i, 1), :] = -jnp.sum(jnp.where(eye, wide, 0.0), axis=0, keepdims=True)
+
+    def coupling(i):
         t_copy(i).wait()
         t_re, t_im = tv[i, 0], tv[i, 1]
-        t_cat = jnp.concatenate([t_re, t_im], axis=1)
-        t_swap = jnp.concatenate([-t_im, t_re], axis=1)
-        if first:
-            left = t_cat
-        else:
-            parts = []
-            for e in range(EL):
-                g_re, g_im = rows_of(i - 1, e, 0), rows_of(i - 1, e, 1)
-                p_re = mm(t_cat, jnp.concatenate([g_re, -g_im], axis=0)).astype(BF16)
-                p_im = mm(t_cat, jnp.concatenate([g_im, g_re], axis=0)).astype(BF16)
-                parts.append(jnp.concatenate([p_re, p_im], axis=1))
-            left = jnp.concatenate(parts, axis=0)
+        return jnp.concatenate([t_re, t_im], axis=1), jnp.concatenate([-t_im, t_re], axis=1)
+
+    def first_block(c_re, c_im, quarters):
+        def take(c, e):
+            return jnp.concatenate([av[0, c, e, pl.ds(j * Q, Q)] for j in quarters], axis=0)
+
+        height = len(quarters) * Q
+        own = [(take(0, e), take(1, e)) for e in range(EL)]
+        a_cat = jnp.concatenate([jnp.concatenate(pair, axis=1) for pair in own], axis=0)
+        q_re = mm(a_cat, jnp.concatenate([c_re, -c_im], axis=0)).astype(BF16)
+        q_im = mm(a_cat, jnp.concatenate([c_im, c_re], axis=0)).astype(BF16)
+        for e in range(EL):
+            at = e * height
+            a_re, a_im = av[0, 0, e], av[0, 1, e]
+            q_cat = jnp.concatenate([q_re[at:at + height], q_im[at:at + height]], axis=1)
+            h_re = mm(q_cat, jnp.concatenate([a_re, -a_im], axis=0))
+            h_im = mm(q_cat, jnp.concatenate([a_im, a_re], axis=0))
+            for c, h in ((0, h_re), (1, h_im)):
+                g = (own[e][c].astype(F32) + h).astype(BF16)
+                for n, j in enumerate(quarters):
+                    gb[0, j, e, c] = g[n * Q:(n + 1) * Q]
+
+    def solve(i):
+        t_cat, t_swap = coupling(i)
+        parts = []
+        for e in range(EL):
+            g_re, g_im = rows_of(i - 1, e, 0), rows_of(i - 1, e, 1)
+            p_re = mm(t_cat, jnp.concatenate([g_re, -g_im], axis=0)).astype(BF16)
+            p_im = mm(t_cat, jnp.concatenate([g_im, g_re], axis=0)).astype(BF16)
+            parts.append(jnp.concatenate([p_re, p_im], axis=1))
+        left = jnp.concatenate(parts, axis=0)
         s_re = mm_nt(left, t_cat).astype(BF16)
         s_im = mm_nt(left, t_swap).astype(BF16)
         a_copy(i).wait()
-        trace = None
         for e in range(EL):
-            at = 0 if first else e * B
+            at = e * B
             a_re, a_im = av[i, 0, e], av[i, 1, e]
             c_re, c_im = s_re[at:at + B], s_im[at:at + B]
             a_cat = jnp.concatenate([a_re, a_im], axis=1)
@@ -138,22 +198,28 @@
             q_cat = jnp.concatenate([q_re, q_im], axis=1)
             h_re = mm(q_cat, jnp.concatenate([a_re, -a_im], axis=0))
             h_im = mm(q_cat, jnp.concatenate([a_im, a_re], axis=0))
-            g_re = (a_re.astype(F32) + h_re).astype(BF16)
-            g_im = (a_im.astype(F32) + h_im).astype(BF16)
-            gb[i, :, e, 0] = g_re.reshape(K, Q, B)
-            gb[i, :, e, 1] = g_im.reshape(K, Q, B)
-            wide = g_im.astype(F32)
-            trace = wide if trace is None else trace + wide
-        dens[pl.ds(i, 1), :] = -jnp.sum(jnp.where(eye, trace, 0.0), axis=0, keepdims=True)
+            gb[i, :, e, 0] = (a_re.astype(F32) + h_re).astype(BF16).reshape(K, Q, B)
+            gb[i, :, e, 1] = (a_im.astype(F32) + h_im).astype(BF16).reshape(K, Q, B)
+        note(i)
 
     def ship(i):
         for d in (1, 3, 2):
             gather(i, d).start()
         rb[i, :, me] = gb[i, me]
 
-    solve(0, True)
-    pl.semaphore_wait(barrier, len(greeted))
-    ship(0)
+    t_cat, t_swap = coupling(0)
+    c_re, c_im = mm_nt(t_cat, t_cat).astype(BF16), mm_nt(t_cat, t_swap).astype(BF16)
+    a_copy(0).wait()
+    near = 1 + 2 * lax.rem(me, 2)
+    far = K - near
+    first_block(c_re, c_im, [lax.rem(me + near, K)])
+    ring_ready()
+    gather(0, near).start()
+    first_block(c_re, c_im, [lax.rem(me + far, K), lax.rem(me + 2, K), me])
+    gather(0, far).start()
+    gather(0, 2).start()
+    rb[0, :, me] = gb[0, me]
+    note(0)
 
     for n, (source, target) in enumerate(small):
         pltpu.make_async_copy(source, target, small_sem.at[n]).wait()
@@ -192,11 +258,12 @@
             lmat[128 + at:128 + at + 16, :] = (tile - top.astype(F32)).astype(BF16)
 
     def chain(i, carry):
-        solve(i, False)
+        solve(i)
         ship(i)
         return carry
 
     lax.fori_loop(1, NB, chain, 0)
+    outside_ready()
 
     stages = [[mom_peer(d) for d in (1, 2, 3)], [twin], [z_peer(d) for d in (1, 2, 3)], [x_peer(d) for d in (1, 2, 3)]]
 
@@ -338,6 +405,7 @@
             dma((NB, 3)), dma((NB, 3)),
             dma((NB,)),
             dma((4, 3)), dma((4, 3)),
+            pltpu.SemaphoreType.REGULAR,
         ],
         compiler_params=pltpu.CompilerParams(
             collective_id=0, has_side_effects=True, vmem_limit_bytes=48 << 20),

time: 103 us -> 103 us (level); the launches traced: 101 us -> 103 us
    pallas_call x1, Pallas kernels: 98.7 us -> 99.9 us  [body(): pl.pallas_call(kernel, out_shape=(jax.ShapeDtypeStruct(inverse_blocks.sha...]
where the time goes in v4:
time: 103 us
  Pallas kernels  102 us (99%)
    pallas_call x1, Pallas kernels, body(): pl.pallas_call(kernel, out_shape=(jax.ShapeDtypeStruct(inverse_blocks.sha...  99.9 us
    pallas_call x1, Pallas kernels, body(): pl.pallas_call(place, out_shape=(jax.ShapeDtypeStruct(landed.shape, BF16)...  2.12 us

profile of v4, /device:TPU:1, one launch (start us, length us, event | category | flops | bytes accessed | tf_op | source)
XLA Modules:
  0.0 102.6 jit_solution(16337949321418729808)
XLA Ops:
  0.6 99.9 %shard_map.86 = (bf16[2,2,1,2048,256]{4,3,2,1,0:T(8,128)(2,1)S(1)}, f32[1,128]{1,0:T(1,128)S(1)}) custom-call(bf16[2,2,1,2048,256]{4,3,2,1,0:T(8,128)(2,1)} %a_hbm.1, bf16[2,1,2048,256]{3,2,1,0:T(8,128)(2,1)} %t_hbm.1, f32[2048]{0:T(1024)} %d_hbm.1, s32[4]{0:T(128)} %shifts_hbm.1, f32[4,4,4]{2,1,0:T(4,128)} %emission_hbm.1, f32[4,4,4]{2,1,0:T(4,128)} %absorption_hbm.1, ...), custom_call_target="tpu_custom_call" | custom-call | tf_op jit(solution)/shard_map/pallas_call | solution.py:376
  100.5 2.1 %shard_map.87 = (bf16[2,2,1,2048,256]{4,3,2,1,0:T(8,128)(2,1)}, f32[1]{0:T(128)}) custom-call(bf16[2,2,1,2048,256]{4,3,2,1,0:T(8,128)(2,1)S(1)} %get-tuple-element.4.landed, f32[1]{0:T(128)S(1)} %bitcast.2), custom_call_target="tpu_custom_call" | custom-call | tf_op jit(solution)/shard_map/pallas_call | solution.py:413

commit v5 on v4

--- a/solution.py
+++ b/solution.py
@@ -44,7 +44,7 @@
 
     above, below = (lax.rem(E + 1, NE), me), (lax.rem(E + NE - 1, NE), me)
     twin = (x * 8 + z * 2 + 1 - core, me)
-    COUNTER, ENVOY = 1, 3
+    COUNTER, ENVOY = 0, 1
     is_counter, is_envoy = (me == COUNTER) & (core == 1), (me == ENVOY) & (core == 1)
     home = E - core
     rings = [(x * 8 + lax.rem(z + d, 4) * 2) for d in (1, 2, 3)] + [lax.rem(home + 8 * d, NE) for d in (1, 2, 3)]

time: 103 us -> 102 us (level)
    pallas_call x1, Pallas kernels: 99.9 us -> 98.7 us  [body(): pl.pallas_call(kernel, out_shape=(jax.ShapeDtypeStruct(inverse_blocks.sha...]
where the time goes in v5:
time: 102 us; the launch traced here: 101 us
  Pallas kernels  101 us (99%)
    pallas_call x1, Pallas kernels, body(): pl.pallas_call(kernel, out_shape=(jax.ShapeDtypeStruct(inverse_blocks.sha...  98.7 us
    pallas_call x1, Pallas kernels, body(): pl.pallas_call(place, out_shape=(jax.ShapeDtypeStruct(landed.shape, BF16)...  2.12 us

profile of v5, /device:TPU:1, one launch (start us, length us, event | category | flops | bytes accessed | tf_op | source)
XLA Modules:
  0.0 101.4 jit_solution(14613224145381260230)
XLA Ops:
  0.6 98.7 %shard_map.86 = (bf16[2,2,1,2048,256]{4,3,2,1,0:T(8,128)(2,1)S(1)}, f32[1,128]{1,0:T(1,128)S(1)}) custom-call(bf16[2,2,1,2048,256]{4,3,2,1,0:T(8,128)(2,1)} %a_hbm.1, bf16[2,1,2048,256]{3,2,1,0:T(8,128)(2,1)} %t_hbm.1, f32[2048]{0:T(1024)} %d_hbm.1, s32[4]{0:T(128)} %shifts_hbm.1, f32[4,4,4]{2,1,0:T(4,128)} %emission_hbm.1, f32[4,4,4]{2,1,0:T(4,128)} %absorption_hbm.1, ...), custom_call_target="tpu_custom_call" | custom-call | tf_op jit(solution)/shard_map/pallas_call | solution.py:376
  99.3 2.1 %shard_map.87 = (bf16[2,2,1,2048,256]{4,3,2,1,0:T(8,128)(2,1)}, f32[1]{0:T(128)}) custom-call(bf16[2,2,1,2048,256]{4,3,2,1,0:T(8,128)(2,1)S(1)} %get-tuple-element.4.landed, f32[1]{0:T(128)S(1)} %bitcast.2), custom_call_target="tpu_custom_call" | custom-call | tf_op jit(solution)/shard_map/pallas_call | solution.py:413
